TPU v7x, 512 devices: a whole 4x4x16 slice. The times are simulated.
512 devices in a mesh: depth: 32 (over y_hi, z), src: 16 (over x, y_lo, core).
Axes of the slice: x: 4, y: 4 (y_hi: 2, y_lo: 2; y = y_hi * 2 + y_lo), z: 16, core: 2. Of those that a mesh axis runs over, the one named last changes fastest.
Arguments:
- forward: bfloat16 [32, 128, 128, 128], P('src', 'depth'), may hold values from 0.099609375 to 3
- detectors: int32 [524288], P('depth'), may hold values from 0 to 65535, as said below
- residuals: float32 [32, 524288], P('src', 'depth'), may hold values from -6 to 6
- delay_index: int32 [32], P('src'), may hold values from 0 to 7
- labels: int32 [128, 128, 128], P('depth'), may hold values from 0 to 4
- blood_flow: float32 [128, 128, 128], P('depth'), may hold values from 0.2 to 5
- diff_table: float32 [5], replicated, may hold values from 0.5 to 1.5
- absorb_table: float32 [5], replicated, may hold values from 0.05 to 0.5
- delay_tau: float32 [8], replicated, may hold values from 0.1 to 1
- delay_weight: float32 [8], replicated, may hold values from 0.5 to 2
Outputs:
- gradient: float32 [128, 128, 128], P('depth', 'src')
Inputs may be any that keep to these rules, and one draw needn't show every extreme that they name: `detectors`: detectors 16384 * j to 16384 * (j + 1) - 1 belong to the depth slab of planes 4 * j to 4 * (j + 1) - 1, and each holds a flat index within that slab (z - 4 * j) * 128 * 128 + y * 128 + x; the first of each such block is 0 and the last is 65535; voxels may repeat.
All inputs are finite; a program needn't handle non-finite values.
Results may differ from a plain program's by a relative error of at most 0.00035.
Values sent between devices are 32-bit elements; how exact they have to be, the bound alone decides.
A program may use at most 128 MiB of HBM per device.

v0:
```python
import jax
import jax.numpy as jnp
from jax import lax
from jax.sharding import PartitionSpec as P

CHEB = 3


SPECTRUM_LOW = 0.1
SPECTRUM_HIGH = 2.0


def extended(value, sides, width):
    for axis, dim in sides:
        devices, length = (lax.axis_size(axis), value.shape[dim])
        up = [(i, (i + 1) % devices) for i in range(devices - 1)]
        down = [(j, i) for i, j in up]
        last = lax.slice_in_dim(value, length - width, length, axis=dim)
        initial = lax.slice_in_dim(value, 0, width, axis=dim)
        before = lax.ppermute(last, axis, up)
        after = lax.ppermute(initial, axis, down)
        value = jnp.concatenate([before, value, after], axis=dim)
    return value


def lookup(values_table, label_keys):
    result = jnp.zeros(label_keys.shape, jnp.float32)
    for entry in range(values_table.shape[0]):
        result = result + jnp.where(label_keys == entry, values_table[entry], jnp.float32(0.0))
    return result


def neighbor(array, which_axis, offset):
    window = [slice(1, array.shape[array.ndim - 3 + spatial] - 1) for spatial in range(3)]
    extent = array.shape[array.ndim - 3 + which_axis]
    window[which_axis] = slice(offset, extent - 2 + offset)
    leading = tuple((slice(None) for leading_dim in range(array.ndim - 3)))
    return array[leading + tuple(window)]


def operate(field_pad, diffusion_pad, absorb):
    centre_field = neighbor(field_pad, 0, 1)
    centre_diff = neighbor(diffusion_pad, 0, 1)
    result = absorb * centre_field
    for which_axis in range(3):
        for offset in (0, 2):
            face_coef = 0.5 * (centre_diff + neighbor(diffusion_pad, which_axis, offset))
            result = result + face_coef * (centre_field - neighbor(field_pad, which_axis, offset))
    return result


def diagonal(diffusion_pad, absorb):
    centre_diff = neighbor(diffusion_pad, 0, 1)
    result = absorb
    for which_axis in range(3):
        for offset in (0, 2):
            result = result + 0.5 * (centre_diff + neighbor(diffusion_pad, which_axis, offset))
    return result


def chebyshev(source_term, diagonal_terms, apply_fn, keep_fn):
    centre = 0.5 * (SPECTRUM_HIGH + SPECTRUM_LOW)
    half_width = 0.5 * (SPECTRUM_HIGH - SPECTRUM_LOW)
    ratio_sigma = centre / half_width
    rho_prev = 1.0 / ratio_sigma
    step_field = keep_fn(source_term / diagonal_terms / centre)
    iterate = step_field
    residual = source_term
    for turn in range(1, CHEB):
        residual = residual - apply_fn(step_field)
        rho_now = 1.0 / (2.0 * ratio_sigma - rho_prev)
        step_field = keep_fn(
            rho_now * rho_prev * step_field
            + 2.0 * rho_now / half_width * (residual / diagonal_terms)
        )
        iterate = iterate + step_field
        rho_prev = rho_now
    return iterate


def identity_keep(step_field):
    return step_field


def body(
    forward,
    detectors,
    residuals,
    delay_index,
    labels,
    blood_flow,
    diff_table,
    absorb_table,
    delay_tau,
    delay_weight,
):
    slab_depth, rows_y, cols_x = labels.shape
    slab_cells = slab_depth * rows_y * cols_x
    pair_count = forward.shape[0]
    coef_margin = 1
    source_term = jnp.zeros((pair_count, slab_cells), jnp.float32).at[:, detectors].add(residuals)
    source_term = source_term.reshape(pair_count, slab_depth, rows_y, cols_x)
    stacked = jnp.stack([lookup(diff_table, labels), lookup(absorb_table, labels), blood_flow])
    widened = extended(stacked, (("depth", 1),), coef_margin)
    diffusion = widened[0]
    base_absorb = widened[1]
    flow_wide = widened[2]
    diffusion_pad = jnp.pad(diffusion, ((0, 0), (1, 1), (1, 1)))
    pair_tau = lookup(delay_tau, delay_index)
    pair_weight = lookup(delay_weight, delay_index)
    absorb = base_absorb[None, 1:-1] + pair_tau[:, None, None, None] * flow_wide[None, 1:-1]
    diagonal_terms = diagonal(diffusion_pad, absorb)

    def apply_fn(step_field):
        padded = extended(step_field, (("depth", 1),), 1)
        padded = jnp.pad(padded, ((0, 0), (0, 0), (1, 1), (1, 1)))
        return operate(padded, diffusion_pad, absorb)

    adjoint = chebyshev(source_term, diagonal_terms, apply_fn, identity_keep)
    pair_coef = -(pair_weight * pair_tau)
    gradient_sum = jnp.sum(
        pair_coef[:, None, None, None] * forward.astype(jnp.float32) * adjoint, axis=0
    )
    return lax.psum_scatter(gradient_sum, "src", scatter_dimension=1, tiled=True)


def solution(mesh):
    placed = (
        P("src", "depth", None, None),
        P("depth"),
        P("src", "depth"),
        P("src"),
        P("depth", None, None),
        P("depth", None, None),
        P(),
        P(),
        P(),
        P(),
    )
    return jax.shard_map(
        body, mesh=mesh, in_specs=placed, out_specs=P("depth", "src", None), check_vma=False
    )
```

profile of v0, /device:TPU:32, one launch (start us, length us, event | category | flops | bytes accessed | tf_op | source)
XLA Modules:
  0.0 273.7 jit_solution(13629016044742595703)
XLA Ops:
  6.6 1.5 fusion.80
  8.1 1.5 fusion.79
  9.6 4.4 %fusion.73 = (f32[1,4,128,128]{3,2,1,0:T(8,128)S(1)}, pred[4,128,128]{2,1,0:T(8,128)(4,1)S(1)}, pred[4,128,128]{2,1,0:T(8,128)(4,1)S(1)}, pred[4,128,128]{2,1,0:...) fusion(f32[]{:T(128)} %bitcast.27, f32[]{:T(128)} %bitcast.26, f32[]{:T(128)} %bitcast.25, ...), kind=kLoop, calls=%fused_computation.139 | loop fusion | flops 917504 | bytes 851988 | tf_op jit(solution)/shard_map/stack | solution.py:103
  14.0 3.4 %select_add_fusion.1 = f32[4,128,128]{2,1,0:T(8,128)S(1)} fusion(pred[4,128,128]{2,1,0:T(8,128)(4,1)S(1)} %get-tuple-element.12, pred[4,128,128]{2,1,0:T(8,128)(4,1)S(1)} %get-tuple-element.11, pred[4,128,128]{2,1,0:T(8,128)(4,1)S(1)} %get-tuple-element.10, pred[4,128,128]{2,1,0:T(8,128)(4,1)S(1)} %get-tuple-element.9, ...), kind=kLoop, calls=%fused_computation.97 | loop fusion | flops 589824 | bytes 589844 | tf_op jit(solution)/shard_map/add | solution.py:29
  17.4 3.8 %collective-permute-start = (f32[3,1,128,128]{3,2,1,0:T(8,128)S(1)}, f32[3,1,128,128]{3,2,1,0:T(8,128)S(1)}, u32[]{:S(2)}, u32[]{:S(2)}) collective-permute-start(f32[3,1,128,128]{3,2,1,0:T(8,128)S(1)} %get-tuple-element.15), channel_id=1, source_target_pairs={{0,16},{16,32},{32,48},{48,64},{64,80},{80,96},{96,112},{112,128},... | collective-permute-start | bytes 589832 | tf_op jit(solution)/shard_map/ppermute | solution.py:20
  21.2 4.8 %collective-permute-start.1 = (f32[3,1,128,128]{3,2,1,0:T(8,128)S(1)}, f32[3,1,128,128]{3,2,1,0:T(8,128)S(1)}, u32[]{:S(2)}, u32[]{:S(2)}) collective-permute-start(f32[3,1,128,128]{3,2,1,0:T(8,128)S(1)} %get-tuple-element.16), channel_id=1, source_target_pairs={{16,0},{32,16},{48,32},{64,48},{80,64},{96,80},{112,96},{128,112},... | collective-permute-start | bytes 589832 | tf_op jit(solution)/shard_map/ppermute | solution.py:21
  26.1 0.7 fusion.77
  26.8 0.7 fusion.78
  27.5 4.9 %copy.11 = f32[16384,2]{1,0:T(8,128)} copy(f32[16384,2]{0,1:T(2,128)S(1)} %bitcast.53) | data formatting | bytes 262144 | tf_op args[2]
  32.4 100.8 %scatter_custom_fusion = f32[2,65536]{0,1:T(8,128)} fusion(s32[16384]{0:T(1024)S(1)} %compare_select_fusion, f32[16384,2]{1,0:T(8,128)} %copy.11, f32[]{:T(128)} %constant.17.clone.1), kind=kCustom, calls=%fused_computation.1 | custom fusion | flops 32768 | bytes 524800 | tf_op jit(solution)/shard_map/scatter-add | solution.py:101
  133.2 19.5 %copy.12 = f32[2,4,128,128]{3,2,1,0:T(8,128)S(1)} copy(f32[2,4,128,128]{0,3,2,1:T(8,128)} %bitcast.46) | data formatting | bytes 1048576 | tf_op jit(solution)/shard_map/reshape | solution.py:102
  152.7 9.9 %fusion.72 = (f32[2]{0:T(128)S(1)}, f32[2]{0:T(128)S(1)}) fusion(s32[2]{0:T(128)S(1)} %copy-done.6, f32[]{:T(128)} %bitcast.7, f32[]{:T(128)} %bitcast.6, f32[]{:T(128)} %bitcast.5, f32[]{:T(128)} %bitcast.4, f32[]{:T(128)} %bitcast.3, f32[]{:T(128)} %bitcast.2, f32[]{:T(128)} %bitcast.1, f32[]{:T(128)} %bitcast, f32[]{:T(128)} %bitcast.15, f32[]{:T(128)} %bitcast.14, ...), kind=kLoop, calls=%fused_computation.138 | loop fusion | flops 80 | bytes 88 | tf_op jit(solution)/shard_map/neg | solution.py:120
  162.6 3.5 %fusion.44 = (f32[4,128,128]{2,1,0:T(8,128)S(1)}, f32[4,128,128]{2,1,0:T(8,128)S(1)}, f32[4,128,128]{2,1,0:T(8,128)S(1)}, f32[4,128,128]{2,1,0:T(8,128)S(1)}) fusion(f32[6,128,128]{2,1,0:T(8,128)S(1)} %fusion.42, pred[4,128,128]{2,1,0:T(8,128)(4,1)S(1)} %get-tuple-element.12, f32[]{:T(128)} %bitcast.27, pred[4,128,128]{2,1,0:T(8,128)(4,1)S(1)} %get-tuple-element.11, ...), kind=kLoop, calls=%fused_computation.76 | loop fusion | flops 1114112 | bytes 1769492 | tf_op jit(solution)/shard_map/mul | solution.py:57
  166.1 3.4 %fusion.56 = (f32[4,128,128]{2,1,0:T(8,128)S(1)}, f32[4,128,128]{2,1,0:T(8,128)S(1)}) fusion(f32[3,1,128,128]{3,2,1,0:T(8,128)S(1)} %collective-permute-done, f32[1,4,128,128]{3,2,1,0:T(8,128)S(1)} %bitcast.52, f32[1,4,128,128]{3,2,1,0:T(8,128)S(1)} %bitcast.49, f32[1,4,128,128]{3,2,1,0:T(8,128)S(1)} %get-tuple-element.7, ...), kind=kLoop, calls=%fused_computation.92 | loop fusion | flops 1245184 | bytes 2031636 | tf_op jit(solution)/shard_map/mul | solution.py:57
  169.8 1.9 collective-permute-start.2
  171.7 3.9 %collective-permute-start.3 = (f32[2,1,128,128]{3,2,1,0:T(8,128)S(1)}, f32[2,1,128,128]{3,2,1,0:T(8,128)S(1)}, u32[]{:S(2)}, u32[]{:S(2)}) collective-permute-start(f32[2,1,128,128]{3,2,1,0:T(8,128)S(1)} %get-tuple-element.24), channel_id=1, source_target_pairs={{16,0},{32,16},{48,32},{64,48},{80,64},{96,80},{112,96},{128,112},... | collective-permute-start | bytes 393224 | tf_op jit(solution)/shard_map/ppermute | solution.py:21
  175.7 1.0 collective-permute-done.2
  176.7 2.0 collective-permute-done.3
  179.2 0.8 multiply_add_fusion
  180.1 5.3 %collective-permute-start.4 = (f32[2,1,128,128]{3,2,1,0:T(8,128)S(1)}, f32[2,1,128,128]{3,2,1,0:T(8,128)S(1)}, u32[]{:S(2)}, u32[]{:S(2)}) collective-permute-start(f32[2,1,128,128]{3,2,1,0:T(8,128)S(1)} %get-tuple-element.21), channel_id=1, source_target_pairs={{0,16},{16,32},{32,48},{48,64},{64,80},{80,96},{96,112},{112,128},... | collective-permute-start | bytes 393224 | tf_op jit(solution)/shard_map/ppermute | solution.py:20
  185.3 1.9 collective-permute-start.5
  187.8 5.6 %collective-permute-done.5 = f32[2,1,128,128]{3,2,1,0:T(8,128)S(1)} collective-permute-done((f32[2,1,128,128]{3,2,1,0:T(8,128)S(1)}, f32[2,1,128,128]{3,2,1,0:T(8,128)S(1)}, u32[]{:S(2)}, u32[]{:S(2)}) %collective-permute-start.5) | collective-permute-done | bytes 131104 | tf_op jit(solution)/shard_map/ppermute | solution.py:21
  193.9 2.4 fusion.41
  196.3 70.6 %reduce-scatter.2.cloned.1.call-done = f32[4,8,128]{2,1,0:T(8,128)} async-done(((f32[4,128,128]{2,1,0:T(8,128)}), f32[4,8,128]{2,1,0:T(8,128)}) %reduce-scatter.2.cloned.1.call-update) | async-done | bytes 16400 | tf_op jit(solution)/shard_map/reduce_scatter | solution.py:124
  (27 shorter events, 2.0 us)
Async XLA Ops:
  6.5 10.8 %copy-start = (f32[4,128,128]{2,1,0:T(8,128)S(1)}, f32[4,128,128]{2,1,0:T(8,128)}, u32[]{:S(2)}) copy-start(f32[4,128,128]{2,1,0:T(8,128)} %param.15) | copy-start | bytes 786436
  6.5 19.6 %copy-start.4 = (f32[8]{0:T(128)S(1)}, f32[8]{0:T(128)}, u32[]{:S(2)}) copy-start(f32[8]{0:T(128)} %param.18) | copy-start | bytes 100
  6.5 20.2 %copy-start.5 = (f32[8]{0:T(128)S(1)}, f32[8]{0:T(128)}, u32[]{:S(2)}) copy-start(f32[8]{0:T(128)} %param.19) | copy-start | bytes 100
  6.5 20.9 %copy-start.3 = (s32[16384]{0:T(1024)S(1)}, s32[16384]{0:T(1024)}, u32[]{:S(2)}) copy-start(s32[16384]{0:T(1024)} %param.11) | copy-start | bytes 196612
  6.5 20.9 %copy-start.2 = (f32[2,16384]{1,0:T(2,128)S(1)}, f32[2,16384]{1,0:T(2,128)}, u32[]{:S(2)}) copy-start(f32[2,16384]{1,0:T(2,128)} %param.12) | copy-start | bytes 393220
  6.5 260.3 %reduce-scatter.2.cloned.1.call-start = ((), (), s32[]{:S(2)}) async-start(), calls=%async_computation.1 | async-start | bytes 278528 | tf_op jit(solution)/shard_map/reduce_scatter | solution.py:124
  17.4 145.1 %collective-permute-start = (f32[3,1,128,128]{3,2,1,0:T(8,128)S(1)}, f32[3,1,128,128]{3,2,1,0:T(8,128)S(1)}, u32[]{:S(2)}, u32[]{:S(2)}) collective-permute-start(f32[3,1,128,128]{3,2,1,0:T(8,128)S(1)} %get-tuple-element.15), channel_id=1, source_target_pairs={{0,16},{16,32},{32,48},{48,64},{64,80},{80,96},{96,112},{112,128},... | collective-permute-start | bytes 589832 | tf_op jit(solution)/shard_map/ppermute | solution.py:20
  21.2 141.3 %collective-permute-start.1 = (f32[3,1,128,128]{3,2,1,0:T(8,128)S(1)}, f32[3,1,128,128]{3,2,1,0:T(8,128)S(1)}, u32[]{:S(2)}, u32[]{:S(2)}) collective-permute-start(f32[3,1,128,128]{3,2,1,0:T(8,128)S(1)} %get-tuple-element.16), channel_id=1, source_target_pairs={{16,0},{32,16},{48,32},{64,48},{80,64},{96,80},{112,96},{128,112},... | collective-permute-start | bytes 589832 | tf_op jit(solution)/shard_map/ppermute | solution.py:21
  133.2 19.5 %copy-start.6 = (s32[2]{0:T(128)S(1)}, s32[2]{0:T(128)}, u32[]{:S(2)}) copy-start(s32[2]{0:T(128)} %param.13) | copy-start | bytes 28
  169.8 6.9 %collective-permute-start.2 = (f32[2,1,128,128]{3,2,1,0:T(8,128)S(1)}, f32[2,1,128,128]{3,2,1,0:T(8,128)S(1)}, u32[]{:S(2)}, u32[]{:S(2)}) collective-permute-start(f32[2,1,128,128]{3,2,1,0:T(8,128)S(1)} %get-tuple-element.23), channel_id=1, source_target_pairs={{0,16},{16,32},{32,48},{48,64},{64,80},{80,96},{96,112},{112,128},... | collective-permute-start | bytes 393224 | tf_op jit(solution)/shard_map/ppermute | solution.py:20
  171.7 7.0 %collective-permute-start.3 = (f32[2,1,128,128]{3,2,1,0:T(8,128)S(1)}, f32[2,1,128,128]{3,2,1,0:T(8,128)S(1)}, u32[]{:S(2)}, u32[]{:S(2)}) collective-permute-start(f32[2,1,128,128]{3,2,1,0:T(8,128)S(1)} %get-tuple-element.24), channel_id=1, source_target_pairs={{16,0},{32,16},{48,32},{64,48},{80,64},{96,80},{112,96},{128,112},... | collective-permute-start | bytes 393224 | tf_op jit(solution)/shard_map/ppermute | solution.py:21
  180.0 13.9 %copy-start.1 = (bf16[2,4,128,128]{3,2,1,0:T(8,128)(2,1)S(1)}, bf16[2,4,128,128]{3,2,1,0:T(8,128)(2,1)}, u32[]{:S(2)}) copy-start(bf16[2,4,128,128]{3,2,1,0:T(8,128)(2,1)} %param.10) | copy-start | bytes 786436
  180.1 7.8 %collective-permute-start.4 = (f32[2,1,128,128]{3,2,1,0:T(8,128)S(1)}, f32[2,1,128,128]{3,2,1,0:T(8,128)S(1)}, u32[]{:S(2)}, u32[]{:S(2)}) collective-permute-start(f32[2,1,128,128]{3,2,1,0:T(8,128)S(1)} %get-tuple-element.21), channel_id=1, source_target_pairs={{0,16},{16,32},{32,48},{48,64},{64,80},{80,96},{96,112},{112,128},... | collective-permute-start | bytes 393224 | tf_op jit(solution)/shard_map/ppermute | solution.py:20
  185.3 8.1 %collective-permute-start.5 = (f32[2,1,128,128]{3,2,1,0:T(8,128)S(1)}, f32[2,1,128,128]{3,2,1,0:T(8,128)S(1)}, u32[]{:S(2)}, u32[]{:S(2)}) collective-permute-start(f32[2,1,128,128]{3,2,1,0:T(8,128)S(1)} %get-tuple-element.22), channel_id=1, source_target_pairs={{16,0},{32,16},{48,32},{64,48},{80,64},{96,80},{112,96},{128,112},... | collective-permute-start | bytes 393224 | tf_op jit(solution)/shard_map/ppermute | solution.py:21
Sparse Core Ops, SparseCore 0:
  196.5 70.3 reduce-scatter.1
where the time goes:
time: 275 us; the launch traced here: 274 us
  other arithmetic  130 us (47%)
  waiting for transfers between devices  79.8 us (29%)
  local copies, waits for them, and re-layouts  28.8 us (10%)
  starting transfers between devices  21.7 us (8%)
  between operations  13.6 us (5%)
    scatter-add x1, other arithmetic, body(): jnp.zeros((pair_count, slab_cells), jnp.float32).at[:, detectors]  101 us
    reduce_scatter x1, waiting for transfers between devices, body(): lax.psum_scatter(gradient_sum, 'src', scatter_dimension=1, tiled=True)  70.6 us
    reshape x1, local copies, waits for them, and re-layouts, body(): source_term = source_term.reshape(pair_count, slab_depth, rows_y, cols_x)  19.5 us
    ppermute x3, starting transfers between devices, extended(): before = lax.ppermute(last, axis, up)  11 us
    ppermute x3, starting transfers between devices, extended(): after = lax.ppermute(initial, axis, down)  10.7 us
    neg x1, other arithmetic, body(): pair_coef = -(pair_weight * pair_tau)  9.88 us
    ppermute x3, waiting for transfers between devices, extended(): after = lax.ppermute(initial, axis, down)  7.6 us
    mul x2, other arithmetic, diagonal(): 0.5 * (centre_diff + neighbor(diffusion_pad, which_axis, offset))  6.88 us
  transfers between devices with their start and end apart: 7, of which 5 were waited for; matrix products, arithmetic and copies ran while one was open for 50% of the time, Pallas kernels for 0%

commit v1 on v0

v1 whole, which is shorter than its diff:
```python
import functools

import jax
import jax.numpy as jnp
from jax import lax
from jax.experimental import pallas as pl
from jax.experimental.pallas import tpu as pltpu
from jax.sharding import PartitionSpec as P

SPECTRUM_LOW = 0.1
SPECTRUM_HIGH = 2.0
CENTRE = 0.5 * (SPECTRUM_HIGH + SPECTRUM_LOW)
HALF = 0.5 * (SPECTRUM_HIGH - SPECTRUM_LOW)
SIGMA = CENTRE / HALF
RHO0 = 1.0 / SIGMA
RHO1 = 1.0 / (2.0 * SIGMA - RHO0)
RHO2 = 1.0 / (2.0 * SIGMA - RHO1)

N = 128
CHUNK = 1024
MESH = pl.DeviceIdType.MESH
F32 = jnp.float32
BF16 = jnp.bfloat16


def lookup(table, labels, count):
    value = jnp.zeros(labels.shape, F32)
    for entry in range(count):
        value = jnp.where(labels == entry, table[entry], value)
    return value


def kernel(
    groups, depths,
    fwd, det, res, labels, flow, index, dtab, atab, tau, wgt,
    out,
    rt, acc, lab_h, diff, inv, gx, gy, gz, d0, d1, q1, d0h, d1h, part, recv,
    lab_s, lab_r, d0_s, d0_r, d1_s, d1_r, rs_s, rs_r,
):
    me = lax.axis_index("src")
    z = lax.axis_index("depth")
    up = lax.rem(z + 1, depths)
    down = lax.rem(z + depths - 1, depths)
    first = z == 0
    last = z == depths - 1
    pairs, planes = fwd.shape[0], fwd.shape[1]
    count = det.shape[1]

    barrier = pltpu.get_barrier_semaphore()
    for side in (up, down):
        pl.semaphore_signal(barrier, inc=1, device_id={"depth": side}, device_id_type=MESH)
    for step in range(1, groups):
        peer = lax.rem(me + step, groups)
        pl.semaphore_signal(barrier, inc=1, device_id={"src": peer}, device_id_type=MESH)

    row16 = lax.broadcasted_iota(jnp.int32, (16, CHUNK), 0).astype(F32)
    ids = [(row16 + 16.0 * b).astype(BF16) for b in range(N // 16)]
    zero = jnp.zeros((16, CHUNK), BF16)
    one = jnp.ones((16, CHUNK), BF16)

    def spread(row):
        return jnp.broadcast_to(row, (16, CHUNK)).astype(BF16)

    def rows_of(detectors, plane):
        mine = spread(((detectors >> 7) - plane * N).astype(F32))
        return [jnp.where(mine == ids[b], one, zero) for b in range(N // 16)]

    def select(chunk, wanted, fresh):
        start = pl.multiple_of(chunk * CHUNK, CHUNK)
        detectors = det[:, pl.ds(start, CHUNK)]
        if fresh:
            column = spread((detectors & (N - 1)).astype(F32))
            weights = []
            for p in range(pairs):
                value = res[p:p + 1, pl.ds(start, CHUNK)]
                head = value.astype(BF16).astype(F32)
                weights.append((p, spread(head)))
                weights.append((pairs + p, spread(value - head)))
            for b in range(N // 16):
                hit = column == ids[b]
                for slot, weight in weights:
                    rt[slot * N + 16 * b:slot * N + 16 * b + 16, pl.ds(start, CHUNK)] = (
                        jnp.where(hit, weight, zero))
        rows = []
        for plane in wanted:
            rows += rows_of(detectors, plane)
        onehot = jnp.concatenate(rows, axis=0)
        acc[...] += lax.dot_general(
            onehot, rt[:, pl.ds(start, CHUNK)], (((1,), (1,)), ((), ())),
            preferred_element_type=F32)

    def run(begin, end, wanted, fresh):
        def step(chunk, carry):
            select(chunk, wanted, fresh)
            return carry
        lax.fori_loop(begin, end, step, 0)

    def source(slot, p):
        rows = slice(slot * N, (slot + 1) * N)
        return acc[rows, p * N:(p + 1) * N] + acc[rows, (pairs + p) * N:(pairs + p + 1) * N]

    chunks = count // CHUNK
    acc[...] = jnp.zeros_like(acc)
    run(0, chunks // 4, (0, planes - 1), True)

    pl.semaphore_wait(barrier, groups + 1)
    lab_up = pltpu.make_async_remote_copy(
        labels.at[planes - 1], lab_h.at[0], lab_s.at[0], lab_r.at[0],
        device_id={"depth": up}, device_id_type=MESH)
    lab_down = pltpu.make_async_remote_copy(
        labels.at[0], lab_h.at[1], lab_s.at[1], lab_r.at[1],
        device_id={"depth": down}, device_id_type=MESH)
    lab_up.start()
    lab_down.start()

    run(chunks // 4, chunks, (0, planes - 1), True)

    lane = lax.broadcasted_iota(jnp.int32, (N, N), 1)
    row = lax.broadcasted_iota(jnp.int32, (N, N), 0)
    taus = [tau[index[p]] for p in range(pairs)]
    for k in range(planes):
        diff[k] = lookup(dtab, labels[k], dtab.shape[0])
    lab_up.wait()
    lab_down.wait()
    below = jnp.where(first, 0.0, lookup(dtab, lab_h[0], dtab.shape[0]))
    above = jnp.where(last, 0.0, lookup(dtab, lab_h[1], dtab.shape[0]))
    gz[0] = jnp.where(first, 0.0, 0.5 * (below + diff[0]))
    for k in range(1, planes):
        gz[k] = 0.5 * (diff[k - 1] + diff[k])
    gz[planes] = jnp.where(last, 0.0, 0.5 * (diff[planes - 1] + above))
    for k in range(planes):
        here = diff[k]
        right = jnp.where(lane < N - 1, pltpu.roll(here, N - 1, 1), 0.0)
        left = jnp.where(lane > 0, pltpu.roll(here, 1, 1), 0.0)
        south = jnp.where(row < N - 1, pltpu.roll(here, N - 1, 0), 0.0)
        north = jnp.where(row > 0, pltpu.roll(here, 1, 0), 0.0)
        gx[k] = jnp.where(lane < N - 1, 0.5 * (here + right), 0.0)
        gy[k] = jnp.where(row < N - 1, 0.5 * (here + south), 0.0)
        under = below if k == 0 else diff[k - 1]
        over = above if k == planes - 1 else diff[k + 1]
        faces = 3.0 * here + 0.5 * ((left + right) + (north + south) + (under + over))
        base = lookup(atab, labels[k], atab.shape[0]) + faces
        for p in range(pairs):
            inv[k, p] = 1.0 / (base + taus[p] * flow[k])

    ends = (0, planes - 1)
    inner = tuple(range(1, planes - 1))

    def begin(slot, k):
        for p in range(pairs):
            d0[k, p] = source(slot, p) * inv[k, p] * (1.0 / CENTRE)

    def exchange(field, halo, send, receive):
        lift = pltpu.make_async_remote_copy(
            field.at[planes - 1], halo.at[0], send.at[0], receive.at[0],
            device_id={"depth": up}, device_id_type=MESH)
        drop = pltpu.make_async_remote_copy(
            field.at[0], halo.at[1], send.at[1], receive.at[1],
            device_id={"depth": down}, device_id_type=MESH)
        lift.start()
        drop.start()
        return lift, drop

    def gather(field, halo, k, p):
        here = field[k, p]
        under = halo[0, p] if k == 0 else field[k - 1, p]
        over = halo[1, p] if k == planes - 1 else field[k + 1, p]
        total = gz[k] * under + gz[k + 1] * over
        fx, fy = gx[k], gy[k]
        total += fx * pltpu.roll(here, N - 1, 1) + pltpu.roll(fx * here, 1, 1)
        total += fy * pltpu.roll(here, N - 1, 0) + pltpu.roll(fy * here, 1, 0)
        return total

    def advance(k):
        for p in range(pairs):
            old = d0[k, p]
            ratio = (CENTRE - 1.0) * old + inv[k, p] * gather(d0, d0h, k, p)
            q1[k, p] = ratio
            d1[k, p] = (RHO1 * RHO0) * old + (2.0 * RHO1 / HALF) * ratio

    def finish(k):
        total = None
        for p in range(pairs):
            old = d1[k, p]
            ratio = q1[k, p] - old + inv[k, p] * gather(d1, d1h, k, p)
            field = d0[k, p] + (1.0 + RHO2 * RHO1) * old + (2.0 * RHO2 / HALF) * ratio
            coef = -(wgt[index[p]] * taus[p])
            term = coef * fwd[p, k].astype(F32) * field
            total = term if total is None else total + term
        return total

    rows_out = N // groups

    def scatter(phase, low, high):
        sent = []
        for step in range(1, groups):
            peer = lax.rem(me + step, groups)
            rows = pl.ds(pl.multiple_of(peer * rows_out, rows_out), rows_out)
            copy = pltpu.make_async_remote_copy(
                part.at[low:high, rows, :], recv.at[step - 1, low:high],
                rs_s.at[phase, step - 1], rs_r.at[phase, step - 1],
                device_id={"src": peer}, device_id_type=MESH)
            copy.start()
            sent.append(copy)
        return sent

    for slot, k in enumerate(ends):
        begin(slot, k)
    sent0 = exchange(d0, d0h, d0_s, d0_r)

    acc[...] = jnp.zeros_like(acc)
    run(0, chunks, inner, False)
    for slot, k in enumerate(inner):
        begin(slot, k)
    for copy in sent0:
        copy.wait()
    for k in ends:
        advance(k)
    sent1 = exchange(d1, d1h, d1_s, d1_r)
    for k in inner:
        advance(k)
    order = inner + ends
    for slot, k in enumerate(inner):
        part[slot] = finish(k)
    sums = scatter(0, 0, len(inner))
    for copy in sent1:
        copy.wait()
    for slot, k in enumerate(ends):
        part[len(inner) + slot] = finish(k)
    sums += scatter(1, len(inner), planes)
    for copy in sums:
        copy.wait()
    own = pl.ds(pl.multiple_of(me * rows_out, rows_out), rows_out)
    for slot, k in enumerate(order):
        total = part[slot, own, :]
        for step in range(groups - 1):
            total = total + recv[step, slot]
        out[k] = total


def body(
    forward, detectors, residuals, delay_index, labels, blood_flow,
    diff_table, absorb_table, delay_tau, delay_weight,
):
    groups = lax.axis_size("src")
    depths = lax.axis_size("depth")
    pairs, planes = forward.shape[0], forward.shape[1]
    count = detectors.shape[0]
    vmem = pl.BlockSpec(memory_space=pltpu.VMEM)
    smem = pl.BlockSpec(memory_space=pltpu.SMEM)
    dma = pltpu.SemaphoreType.DMA
    plane = lambda *lead: pltpu.VMEM(lead + (N, N), F32)
    return pl.pallas_call(
        functools.partial(kernel, groups, depths),
        out_shape=jax.ShapeDtypeStruct((planes, N // groups, N), F32),
        in_specs=[vmem] * 5 + [smem] * 5,
        out_specs=vmem,
        scratch_shapes=[
            pltpu.VMEM((2 * pairs * N, count), BF16),
            pltpu.VMEM((2 * N, 2 * pairs * N), F32),
            pltpu.VMEM((2, N, N), jnp.int32),
            plane(planes),
            plane(planes, pairs),
            plane(planes),
            plane(planes),
            plane(planes + 1),
            plane(planes, pairs),
            plane(planes, pairs),
            plane(planes, pairs),
            plane(2, pairs),
            plane(2, pairs),
            plane(planes),
            pltpu.VMEM((groups - 1, planes, N // groups, N), F32),
            dma((2,)), dma((2,)), dma((2,)), dma((2,)), dma((2,)), dma((2,)),
            dma((2, groups - 1)), dma((2, groups - 1)),
        ],
        compiler_params=pltpu.CompilerParams(collective_id=0, has_side_effects=True),
        name="flow_gradient",
    )(
        forward, detectors.reshape(1, count), residuals, labels, blood_flow,
        delay_index, diff_table, absorb_table, delay_tau, delay_weight,
    )


def solution(mesh):
    placed = (
        P("src", "depth", None, None),
        P("depth"),
        P("src", "depth"),
        P("src"),
        P("depth", None, None),
        P("depth", None, None),
        P(),
        P(),
        P(),
        P(),
    )
    return jax.shard_map(
        body, mesh=mesh, in_specs=placed, out_specs=P("depth", "src", None), check_vma=False
    )
```

time: 275 us -> 44.4 us (0.16)
  the two profiles are of different devices: /device:TPU:32 before, /device:TPU:1 now
where the time goes in v1:
time: 44.4 us; the launch traced here: 44.2 us
  Pallas kernels  42.9 us (97%)
  local copies, waits for them, and re-layouts  1.32 us (3%)
    pallas_call x1, Pallas kernels, body(): pl.pallas_call(functools.partial(kernel, groups, depths), out_shape=jax.S...  42.9 us
    unnamed x1, local copies, waits for them, and re-layouts  1.32 us

profile of v1, /device:TPU:1, one launch (start us, length us, event | category | flops | bytes accessed | tf_op | source)
XLA Modules:
  0.0 44.2 jit_solution(4315493113172883934)
XLA Ops:
  0.0 42.9 %flow_gradient.1 = f32[4,8,128]{2,1,0:T(8,128)} custom-call(bf16[2,4,128,128]{3,2,1,0:T(8,128)(2,1)} %fwd.1, s32[1,16384]{1,0:T(1,128)} %bitcast.1, f32[2,16384]{1,0:T(2,128)} %res.1, s32[4,128,128]{2,1,0:T(8,128)} %labels.1, f32[4,128,128]{2,1,0:T(8,128)} %flow.1, s32[2]{0:T(128)} %index.1, f32[5]{0:T(128)} %dtab.1, f32[5]{0:T(128)} %atab.1, f32[8]{0:T(128)} %tau.1, ...), custom_call_target="tpu_custom_call" | custom-call | tf_op jit(solution)/shard_map/flow_gradient/pallas_call | solution.py:253
  42.9 1.3 %copy.12 = f32[4,8,128]{2,1,0:T(8,128)} copy(f32[4,8,128]{2,1,0:T(8,128)} %flow_gradient.1) | data formatting | bytes 32768

commit v2 on v1

--- a/solution.py
+++ b/solution.py
@@ -17,7 +17,7 @@
 RHO2 = 1.0 / (2.0 * SIGMA - RHO1)
 
 N = 128
-CHUNK = 1024
+CHUNK = 4096
 MESH = pl.DeviceIdType.MESH
 F32 = jnp.float32
 BF16 = jnp.bfloat16
@@ -32,10 +32,11 @@
 
 def kernel(
     groups, depths,
-    fwd, det, res, labels, flow, index, dtab, atab, tau, wgt,
+    fwd_in, det, res, labels_in, flow_in, index, dtab, atab, tau, wgt,
     out,
-    rt, acc, lab_h, diff, inv, gx, gy, gz, d0, d1, q1, d0h, d1h, part, recv,
-    lab_s, lab_r, d0_s, d0_r, d1_s, d1_r, rs_s, rs_r,
+    fwd, labels, flow, rt, acc, lab_h, flow_h, diff, inv, gx, gy, gz,
+    src, src_h, d0, d0_far, d1, q1, part, recv,
+    in_s, lab_s, lab_r, flow_s, flow_r, src_s, src_r, far_s, far_r, rs_s, rs_r,
 ):
     me = lax.axis_index("src")
     z = lax.axis_index("depth")
@@ -52,6 +53,30 @@
     for step in range(1, groups):
         peer = lax.rem(me + step, groups)
         pl.semaphore_signal(barrier, inc=1, device_id={"src": peer}, device_id_type=MESH)
+    loads = [
+        pltpu.make_async_copy(labels_in, labels, in_s.at[0]),
+        pltpu.make_async_copy(flow_in, flow, in_s.at[1]),
+        pltpu.make_async_copy(fwd_in, fwd, in_s.at[2]),
+    ]
+    for copy in loads:
+        copy.start()
+
+    def shift(to_up, from_below, to_down, from_above, send, receive):
+        pair = (
+            pltpu.make_async_remote_copy(
+                to_up, from_below, send.at[0], receive.at[0],
+                device_id={"depth": up}, device_id_type=MESH),
+            pltpu.make_async_remote_copy(
+                to_down, from_above, send.at[1], receive.at[1],
+                device_id={"depth": down}, device_id_type=MESH),
+        )
+        for copy in pair:
+            copy.start()
+        return pair
+
+    def settle(copies):
+        for copy in copies:
+            copy.wait()
 
     row16 = lax.broadcasted_iota(jnp.int32, (16, CHUNK), 0).astype(F32)
     ids = [(row16 + 16.0 * b).astype(BF16) for b in range(N // 16)]
@@ -100,89 +125,66 @@
         return acc[rows, p * N:(p + 1) * N] + acc[rows, (pairs + p) * N:(pairs + p + 1) * N]
 
     chunks = count // CHUNK
+    ends = (0, planes - 1)
+    inner = tuple(range(1, planes - 1))
+    below, above = planes, planes + 1
+
     acc[...] = jnp.zeros_like(acc)
-    run(0, chunks // 4, (0, planes - 1), True)
-
+    run(0, 1, ends, True)
     pl.semaphore_wait(barrier, groups + 1)
-    lab_up = pltpu.make_async_remote_copy(
-        labels.at[planes - 1], lab_h.at[0], lab_s.at[0], lab_r.at[0],
-        device_id={"depth": up}, device_id_type=MESH)
-    lab_down = pltpu.make_async_remote_copy(
-        labels.at[0], lab_h.at[1], lab_s.at[1], lab_r.at[1],
-        device_id={"depth": down}, device_id_type=MESH)
-    lab_up.start()
-    lab_down.start()
-
-    run(chunks // 4, chunks, (0, planes - 1), True)
+    for copy in loads[:2]:
+        copy.wait()
+    sent_labels = shift(
+        labels.at[planes - 2:planes], lab_h.at[0], labels.at[0:2], lab_h.at[1], lab_s, lab_r)
+    sent_flow = shift(
+        flow.at[planes - 1], flow_h.at[0], flow.at[0], flow_h.at[1], flow_s, flow_r)
+    run(1, chunks, ends, True)
+    for slot in range(2):
+        for p in range(pairs):
+            src[slot, p] = source(slot, p)
+    sent_src = shift(src.at[1], src_h.at[0], src.at[0], src_h.at[1], src_s, src_r)
 
     lane = lax.broadcasted_iota(jnp.int32, (N, N), 1)
     row = lax.broadcasted_iota(jnp.int32, (N, N), 0)
     taus = [tau[index[p]] for p in range(pairs)]
-    for k in range(planes):
-        diff[k] = lookup(dtab, labels[k], dtab.shape[0])
-    lab_up.wait()
-    lab_down.wait()
-    below = jnp.where(first, 0.0, lookup(dtab, lab_h[0], dtab.shape[0]))
-    above = jnp.where(last, 0.0, lookup(dtab, lab_h[1], dtab.shape[0]))
-    gz[0] = jnp.where(first, 0.0, 0.5 * (below + diff[0]))
-    for k in range(1, planes):
-        gz[k] = 0.5 * (diff[k - 1] + diff[k])
-    gz[planes] = jnp.where(last, 0.0, 0.5 * (diff[planes - 1] + above))
-    for k in range(planes):
-        here = diff[k]
+
+    def coefficients(k, here, under, over, label, stream):
         right = jnp.where(lane < N - 1, pltpu.roll(here, N - 1, 1), 0.0)
         left = jnp.where(lane > 0, pltpu.roll(here, 1, 1), 0.0)
         south = jnp.where(row < N - 1, pltpu.roll(here, N - 1, 0), 0.0)
         north = jnp.where(row > 0, pltpu.roll(here, 1, 0), 0.0)
         gx[k] = jnp.where(lane < N - 1, 0.5 * (here + right), 0.0)
         gy[k] = jnp.where(row < N - 1, 0.5 * (here + south), 0.0)
-        under = below if k == 0 else diff[k - 1]
-        over = above if k == planes - 1 else diff[k + 1]
         faces = 3.0 * here + 0.5 * ((left + right) + (north + south) + (under + over))
-        base = lookup(atab, labels[k], atab.shape[0]) + faces
-        for p in range(pairs):
-            inv[k, p] = 1.0 / (base + taus[p] * flow[k])
-
-    ends = (0, planes - 1)
-    inner = tuple(range(1, planes - 1))
-
-    def begin(slot, k):
-        for p in range(pairs):
-            d0[k, p] = source(slot, p) * inv[k, p] * (1.0 / CENTRE)
-
-    def exchange(field, halo, send, receive):
-        lift = pltpu.make_async_remote_copy(
-            field.at[planes - 1], halo.at[0], send.at[0], receive.at[0],
-            device_id={"depth": up}, device_id_type=MESH)
-        drop = pltpu.make_async_remote_copy(
-            field.at[0], halo.at[1], send.at[1], receive.at[1],
-            device_id={"depth": down}, device_id_type=MESH)
-        lift.start()
-        drop.start()
-        return lift, drop
-
-    def gather(field, halo, k, p):
+        base = lookup(atab, label, atab.shape[0]) + faces
+        for p in range(pairs):
+            inv[k, p] = 1.0 / (base + taus[p] * stream)
+
+    def gather(field, k, p, lower, upper, under, over):
         here = field[k, p]
-        under = halo[0, p] if k == 0 else field[k - 1, p]
-        over = halo[1, p] if k == planes - 1 else field[k + 1, p]
-        total = gz[k] * under + gz[k + 1] * over
         fx, fy = gx[k], gy[k]
+        total = lower * under + upper * over
         total += fx * pltpu.roll(here, N - 1, 1) + pltpu.roll(fx * here, 1, 1)
         total += fy * pltpu.roll(here, N - 1, 0) + pltpu.roll(fy * here, 1, 0)
         return total
 
-    def advance(k):
-        for p in range(pairs):
-            old = d0[k, p]
-            ratio = (CENTRE - 1.0) * old + inv[k, p] * gather(d0, d0h, k, p)
+    def inside(field, k, p):
+        under = field[below if k == 0 else k - 1, p]
+        over = field[above if k == planes - 1 else k + 1, p]
+        return gather(field, k, p, gz[k], gz[k + 1], under, over)
+
+    def advance(k, p, shared):
+        old = d0[k, p]
+        ratio = (CENTRE - 1.0) * old + inv[k, p] * shared
+        d1[k, p] = (RHO1 * RHO0) * old + (2.0 * RHO1 / HALF) * ratio
+        if k < planes:
             q1[k, p] = ratio
-            d1[k, p] = (RHO1 * RHO0) * old + (2.0 * RHO1 / HALF) * ratio
 
     def finish(k):
         total = None
         for p in range(pairs):
             old = d1[k, p]
-            ratio = q1[k, p] - old + inv[k, p] * gather(d1, d1h, k, p)
+            ratio = q1[k, p] - old + inv[k, p] * inside(d1, k, p)
             field = d0[k, p] + (1.0 + RHO2 * RHO1) * old + (2.0 * RHO2 / HALF) * ratio
             coef = -(wgt[index[p]] * taus[p])
             term = coef * fwd[p, k].astype(F32) * field
@@ -204,32 +206,65 @@
             sent.append(copy)
         return sent
 
-    for slot, k in enumerate(ends):
-        begin(slot, k)
-    sent0 = exchange(d0, d0h, d0_s, d0_r)
+    for k in range(planes):
+        diff[k] = lookup(dtab, labels[k], dtab.shape[0])
+    for k in range(1, planes):
+        gz[k] = 0.5 * (diff[k - 1] + diff[k])
+    for k in inner:
+        coefficients(k, diff[k], diff[k - 1], diff[k + 1], labels[k], flow[k])
 
     acc[...] = jnp.zeros_like(acc)
     run(0, chunks, inner, False)
     for slot, k in enumerate(inner):
-        begin(slot, k)
-    for copy in sent0:
-        copy.wait()
+        for p in range(pairs):
+            d0[k, p] = source(slot, p) * inv[k, p] * (1.0 / CENTRE)
+    sent_far = shift(
+        d0.at[planes - 2], d0_far.at[0], d0.at[1], d0_far.at[1], far_s, far_r)
+
+    settle(sent_labels)
+    settle(sent_flow)
+    halo = [[lookup(dtab, lab_h[s, i], dtab.shape[0]) for i in range(2)] for s in range(2)]
+    low = jnp.where(first, 0.0, halo[0][1])
+    high = jnp.where(last, 0.0, halo[1][0])
+    gz[0] = jnp.where(first, 0.0, 0.5 * (low + diff[0]))
+    gz[planes] = jnp.where(last, 0.0, 0.5 * (diff[planes - 1] + high))
+    coefficients(0, diff[0], low, diff[1], labels[0], flow[0])
+    coefficients(planes - 1, diff[planes - 1], diff[planes - 2], high,
+                 labels[planes - 1], flow[planes - 1])
+    coefficients(below, halo[0][1], halo[0][0], diff[0], lab_h[0, 1], flow_h[0])
+    coefficients(above, halo[1][0], diff[planes - 1], halo[1][1], lab_h[1, 0], flow_h[1])
+    far = (0.5 * (halo[0][0] + halo[0][1]), 0.5 * (halo[1][0] + halo[1][1]))
+    gz[planes + 1] = far[0]
+    gz[planes + 2] = far[1]
+    for slot, k in enumerate(ends):
+        for p in range(pairs):
+            d0[k, p] = src[slot, p] * inv[k, p] * (1.0 / CENTRE)
+    for k in inner:
+        for p in range(pairs):
+            advance(k, p, inside(d0, k, p))
+    settle(sent_src)
+    for side, k in enumerate((below, above)):
+        for p in range(pairs):
+            d0[k, p] = src_h[side, p] * inv[k, p] * (1.0 / CENTRE)
     for k in ends:
-        advance(k)
-    sent1 = exchange(d1, d1h, d1_s, d1_r)
-    for k in inner:
-        advance(k)
+        for p in range(pairs):
+            advance(k, p, inside(d0, k, p))
+    copy = loads[2]
+    copy.wait()
     order = inner + ends
     for slot, k in enumerate(inner):
         part[slot] = finish(k)
     sums = scatter(0, 0, len(inner))
-    for copy in sent1:
-        copy.wait()
+    settle(sent_far)
+    for p in range(pairs):
+        advance(below, p, gather(
+            d0, below, p, gz[planes + 1], gz[0], d0_far[0, p], d0[0, p]))
+        advance(above, p, gather(
+            d0, above, p, gz[planes], gz[planes + 2], d0[planes - 1, p], d0_far[1, p]))
     for slot, k in enumerate(ends):
         part[len(inner) + slot] = finish(k)
     sums += scatter(1, len(inner), planes)
-    for copy in sums:
-        copy.wait()
+    settle(sums)
     own = pl.ds(pl.multiple_of(me * rows_out, rows_out), rows_out)
     for slot, k in enumerate(order):
         total = part[slot, own, :]
@@ -247,31 +282,38 @@
     pairs, planes = forward.shape[0], forward.shape[1]
     count = detectors.shape[0]
     vmem = pl.BlockSpec(memory_space=pltpu.VMEM)
+    hbm = pl.BlockSpec(memory_space=pl.ANY)
     smem = pl.BlockSpec(memory_space=pltpu.SMEM)
     dma = pltpu.SemaphoreType.DMA
     plane = lambda *lead: pltpu.VMEM(lead + (N, N), F32)
     return pl.pallas_call(
         functools.partial(kernel, groups, depths),
         out_shape=jax.ShapeDtypeStruct((planes, N // groups, N), F32),
-        in_specs=[vmem] * 5 + [smem] * 5,
+        in_specs=[hbm, vmem, vmem, hbm, hbm] + [smem] * 5,
         out_specs=vmem,
         scratch_shapes=[
+            pltpu.VMEM((pairs, planes, N, N), BF16),
+            pltpu.VMEM((planes, N, N), jnp.int32),
+            plane(planes),
             pltpu.VMEM((2 * pairs * N, count), BF16),
             pltpu.VMEM((2 * N, 2 * pairs * N), F32),
-            pltpu.VMEM((2, N, N), jnp.int32),
+            pltpu.VMEM((2, 2, N, N), jnp.int32),
+            plane(2),
             plane(planes),
+            plane(planes + 2, pairs),
+            plane(planes + 2),
+            plane(planes + 2),
+            plane(planes + 3),
+            plane(2, pairs),
+            plane(2, pairs),
+            plane(planes + 2, pairs),
+            plane(2, pairs),
+            plane(planes + 2, pairs),
             plane(planes, pairs),
             plane(planes),
-            plane(planes),
-            plane(planes + 1),
-            plane(planes, pairs),
-            plane(planes, pairs),
-            plane(planes, pairs),
-            plane(2, pairs),
-            plane(2, pairs),
-            plane(planes),
             pltpu.VMEM((groups - 1, planes, N // groups, N), F32),
-            dma((2,)), dma((2,)), dma((2,)), dma((2,)), dma((2,)), dma((2,)),
+            dma((3,)), dma((2,)), dma((2,)), dma((2,)), dma((2,)), dma((2,)), dma((2,)),
+            dma((2,)), dma((2,)),
             dma((2, groups - 1)), dma((2, groups - 1)),
         ],
         compiler_params=pltpu.CompilerParams(collective_id=0, has_side_effects=True),

time: 44.4 us -> 39.7 us (0.89)
  Pallas kernels: 42.9 us -> 38.2 us
    pallas_call x1, Pallas kernels: 42.9 us -> 38.2 us  [body(): pl.pallas_call(functools.partial(kernel, groups, depths), out_shape=jax.S...]
where the time goes in v2:
time: 39.7 us; the launch traced here: 39.5 us
  Pallas kernels  38.2 us (96%)
  local copies, waits for them, and re-layouts  1.32 us (3%)
    pallas_call x1, Pallas kernels, body(): pl.pallas_call(functools.partial(kernel, groups, depths), out_shape=jax.S...  38.2 us
    unnamed x1, local copies, waits for them, and re-layouts  1.32 us

profile of v2, /device:TPU:1, one launch (start us, length us, event | category | flops | bytes accessed | tf_op | source)
XLA Modules:
  0.0 39.5 jit_solution(630654109231685863)
XLA Ops:
  0.0 38.2 %flow_gradient.1 = f32[4,8,128]{2,1,0:T(8,128)} custom-call(bf16[2,4,128,128]{3,2,1,0:T(8,128)(2,1)} %fwd_in.1, s32[1,16384]{1,0:T(1,128)} %bitcast.1, f32[2,16384]{1,0:T(2,128)} %res.1, s32[4,128,128]{2,1,0:T(8,128)} %labels_in.1, f32[4,128,128]{2,1,0:T(8,128)} %flow_in.1, s32[2]{0:T(128)} %index.1, f32[5]{0:T(128)} %dtab.1, f32[5]{0:T(128)} %atab.1, ...), custom_call_target="tpu_custom_call" | custom-call | tf_op jit(solution)/shard_map/flow_gradient/pallas_call | solution.py:289
  38.2 1.3 %copy.12 = f32[4,8,128]{2,1,0:T(8,128)} copy(f32[4,8,128]{2,1,0:T(8,128)} %flow_gradient.1) | data formatting | bytes 32768

commit v3 on v2

--- a/solution.py
+++ b/solution.py
@@ -40,16 +40,20 @@
 ):
     me = lax.axis_index("src")
     z = lax.axis_index("depth")
-    up = lax.rem(z + 1, depths)
-    down = lax.rem(z + depths - 1, depths)
+    up = jnp.minimum(z + 1, depths - 1)
+    down = jnp.maximum(z - 1, 0)
     first = z == 0
     last = z == depths - 1
     pairs, planes = fwd.shape[0], fwd.shape[1]
     count = det.shape[1]
 
     barrier = pltpu.get_barrier_semaphore()
-    for side in (up, down):
-        pl.semaphore_signal(barrier, inc=1, device_id={"depth": side}, device_id_type=MESH)
+    inside_low = z > 0
+    inside_high = z < depths - 1
+    for has, side in ((inside_high, up), (inside_low, down)):
+        @pl.when(has)
+        def _(side=side):
+            pl.semaphore_signal(barrier, inc=1, device_id={"depth": side}, device_id_type=MESH)
     for step in range(1, groups):
         peer = lax.rem(me + step, groups)
         pl.semaphore_signal(barrier, inc=1, device_id={"src": peer}, device_id_type=MESH)
@@ -70,13 +74,28 @@
                 to_down, from_above, send.at[1], receive.at[1],
                 device_id={"depth": down}, device_id_type=MESH),
         )
-        for copy in pair:
-            copy.start()
+        pl.when(inside_high)(pair[0].start)
+        pl.when(inside_low)(pair[1].start)
         return pair
 
-    def settle(copies):
-        for copy in copies:
-            copy.wait()
+    def settle_halo(pair):
+        @pl.when(inside_high)
+        def _():
+            pair[0].wait_send()
+            pair[1].wait_recv()
+
+        @pl.when(inside_low)
+        def _():
+            pair[0].wait_recv()
+            pair[1].wait_send()
+
+    for has, side in ((first, 0), (last, 1)):
+        @pl.when(has)
+        def _(side=side):
+            lab_h[side] = jnp.zeros(lab_h.shape[1:], jnp.int32)
+            flow_h[side] = jnp.ones(flow_h.shape[1:], F32)
+            src_h[side] = jnp.zeros(src_h.shape[1:], F32)
+            d0_far[side] = jnp.zeros(d0_far.shape[1:], F32)
 
     row16 = lax.broadcasted_iota(jnp.int32, (16, CHUNK), 0).astype(F32)
     ids = [(row16 + 16.0 * b).astype(BF16) for b in range(N // 16)]
@@ -131,7 +150,8 @@
 
     acc[...] = jnp.zeros_like(acc)
     run(0, 1, ends, True)
-    pl.semaphore_wait(barrier, groups + 1)
+    pl.semaphore_wait(
+        barrier, groups - 1 + jnp.minimum(z, 1) + jnp.minimum(depths - 1 - z, 1))
     for copy in loads[:2]:
         copy.wait()
     sent_labels = shift(
@@ -221,8 +241,8 @@
     sent_far = shift(
         d0.at[planes - 2], d0_far.at[0], d0.at[1], d0_far.at[1], far_s, far_r)
 
-    settle(sent_labels)
-    settle(sent_flow)
+    settle_halo(sent_labels)
+    settle_halo(sent_flow)
     halo = [[lookup(dtab, lab_h[s, i], dtab.shape[0]) for i in range(2)] for s in range(2)]
     low = jnp.where(first, 0.0, halo[0][1])
     high = jnp.where(last, 0.0, halo[1][0])
@@ -242,7 +262,7 @@
     for k in inner:
         for p in range(pairs):
             advance(k, p, inside(d0, k, p))
-    settle(sent_src)
+    settle_halo(sent_src)
     for side, k in enumerate((below, above)):
         for p in range(pairs):
             d0[k, p] = src_h[side, p] * inv[k, p] * (1.0 / CENTRE)
@@ -255,7 +275,7 @@
     for slot, k in enumerate(inner):
         part[slot] = finish(k)
     sums = scatter(0, 0, len(inner))
-    settle(sent_far)
+    settle_halo(sent_far)
     for p in range(pairs):
         advance(below, p, gather(
             d0, below, p, gz[planes + 1], gz[0], d0_far[0, p], d0[0, p]))
@@ -264,7 +284,8 @@
     for slot, k in enumerate(ends):
         part[len(inner) + slot] = finish(k)
     sums += scatter(1, len(inner), planes)
-    settle(sums)
+    for copy in sums:
+        copy.wait()
     own = pl.ds(pl.multiple_of(me * rows_out, rows_out), rows_out)
     for slot, k in enumerate(order):
         total = part[slot, own, :]

time: 39.7 us -> 36.4 us (0.917)
  the two profiles are of different devices: /device:TPU:1 before, /device:TPU:17 now
where the time goes in v3:
time: 36.4 us; the launch traced here: 36.2 us
  Pallas kernels  34.9 us (96%)
  local copies, waits for them, and re-layouts  1.32 us (4%)
    pallas_call x1, Pallas kernels, body(): pl.pallas_call(functools.partial(kernel, groups, depths), out_shape=jax.S...  34.9 us
    unnamed x1, local copies, waits for them, and re-layouts  1.32 us

profile of v3, /device:TPU:17, one launch (start us, length us, event | category | flops | bytes accessed | tf_op | source)
XLA Modules:
  0.0 36.2 jit_solution(10729935663297951408)
XLA Ops:
  0.0 34.9 %flow_gradient.1 = f32[4,8,128]{2,1,0:T(8,128)} custom-call(bf16[2,4,128,128]{3,2,1,0:T(8,128)(2,1)} %fwd_in.1, s32[1,16384]{1,0:T(1,128)} %bitcast.1, f32[2,16384]{1,0:T(2,128)} %res.1, s32[4,128,128]{2,1,0:T(8,128)} %labels_in.1, f32[4,128,128]{2,1,0:T(8,128)} %flow_in.1, s32[2]{0:T(128)} %index.1, f32[5]{0:T(128)} %dtab.1, f32[5]{0:T(128)} %atab.1, ...), custom_call_target="tpu_custom_call" | custom-call | tf_op jit(solution)/shard_map/flow_gradient/pallas_call | solution.py:310
  34.9 1.3 %copy.12 = f32[4,8,128]{2,1,0:T(8,128)} copy(f32[4,8,128]{2,1,0:T(8,128)} %flow_gradient.1) | data formatting | bytes 32768

commit v4 on v3

--- a/solution.py
+++ b/solution.py
@@ -17,7 +17,7 @@
 RHO2 = 1.0 / (2.0 * SIGMA - RHO1)
 
 N = 128
-CHUNK = 4096
+CHUNK = 8192
 MESH = pl.DeviceIdType.MESH
 F32 = jnp.float32
 BF16 = jnp.bfloat16
@@ -36,7 +36,8 @@
     out,
     fwd, labels, flow, rt, acc, lab_h, flow_h, diff, inv, gx, gy, gz,
     src, src_h, d0, d0_far, d1, q1, part, recv,
-    in_s, lab_s, lab_r, flow_s, flow_r, src_s, src_r, far_s, far_r, rs_s, rs_r,
+    in_s, lab_s, lab_r, flow_s, flow_r, src_s, src_r, far_s, far_r, pass_s, pass_r,
+    rs_s, rs_r,
 ):
     me = lax.axis_index("src")
     z = lax.axis_index("depth")
@@ -154,10 +155,15 @@
         barrier, groups - 1 + jnp.minimum(z, 1) + jnp.minimum(depths - 1 - z, 1))
     for copy in loads[:2]:
         copy.wait()
+    half = N // 2
+    mine = pl.ds(pl.multiple_of(lax.rem(me, 2) * half, half), half)
+    twin = me + 1 - 2 * lax.rem(me, 2)
     sent_labels = shift(
-        labels.at[planes - 2:planes], lab_h.at[0], labels.at[0:2], lab_h.at[1], lab_s, lab_r)
+        labels.at[planes - 2:planes, mine], lab_h.at[0, :, mine],
+        labels.at[0:2, mine], lab_h.at[1, :, mine], lab_s, lab_r)
     sent_flow = shift(
-        flow.at[planes - 1], flow_h.at[0], flow.at[0], flow_h.at[1], flow_s, flow_r)
+        flow.at[planes - 1, mine], flow_h.at[0, mine],
+        flow.at[0, mine], flow_h.at[1, mine], flow_s, flow_r)
     run(1, chunks, ends, True)
     for slot in range(2):
         for p in range(pairs):
@@ -234,15 +240,33 @@
         coefficients(k, diff[k], diff[k - 1], diff[k + 1], labels[k], flow[k])
 
     acc[...] = jnp.zeros_like(acc)
-    run(0, chunks, inner, False)
+    run(0, chunks // 2, inner, False)
+    settle_halo(sent_labels)
+    settle_halo(sent_flow)
+    relays = [
+        pltpu.make_async_remote_copy(
+            ref, ref, pass_s.at[slot], pass_r.at[slot],
+            device_id={"src": twin}, device_id_type=MESH)
+        for slot, ref in enumerate((
+            lab_h.at[0, :, mine], flow_h.at[0, mine], lab_h.at[1, :, mine], flow_h.at[1, mine]))
+    ]
+
+    def each_relay(act):
+        for has, pair in ((inside_low, relays[:2]), (inside_high, relays[2:])):
+            @pl.when(has)
+            def _(pair=pair):
+                for copy in pair:
+                    act(copy)
+
+    each_relay(lambda copy: copy.start())
+    run(chunks // 2, chunks, inner, False)
     for slot, k in enumerate(inner):
         for p in range(pairs):
             d0[k, p] = source(slot, p) * inv[k, p] * (1.0 / CENTRE)
     sent_far = shift(
         d0.at[planes - 2], d0_far.at[0], d0.at[1], d0_far.at[1], far_s, far_r)
 
-    settle_halo(sent_labels)
-    settle_halo(sent_flow)
+    each_relay(lambda copy: copy.wait())
     halo = [[lookup(dtab, lab_h[s, i], dtab.shape[0]) for i in range(2)] for s in range(2)]
     low = jnp.where(first, 0.0, halo[0][1])
     high = jnp.where(last, 0.0, halo[1][0])
@@ -334,7 +358,7 @@
             plane(planes),
             pltpu.VMEM((groups - 1, planes, N // groups, N), F32),
             dma((3,)), dma((2,)), dma((2,)), dma((2,)), dma((2,)), dma((2,)), dma((2,)),
-            dma((2,)), dma((2,)),
+            dma((2,)), dma((2,)), dma((4,)), dma((4,)),
             dma((2, groups - 1)), dma((2, groups - 1)),
         ],
         compiler_params=pltpu.CompilerParams(collective_id=0, has_side_effects=True),

time: 36.4 us -> 43 us (1.18)
  Pallas kernels: 34.9 us -> 41.5 us
    pallas_call x1, Pallas kernels: 34.9 us -> 41.5 us  [body(): pl.pallas_call(functools.partial(kernel, groups, depths), out_shape=jax.S...]
where the time goes in v4:
time: 43 us; the launch traced here: 42.8 us
  Pallas kernels  41.5 us (97%)
  local copies, waits for them, and re-layouts  1.32 us (3%)
    pallas_call x1, Pallas kernels, body(): pl.pallas_call(functools.partial(kernel, groups, depths), out_shape=jax.S...  41.5 us
    unnamed x1, local copies, waits for them, and re-layouts  1.32 us

profile of v4, /device:TPU:17, one launch (start us, length us, event | category | flops | bytes accessed | tf_op | source)
XLA Modules:
  0.0 42.8 jit_solution(4987932898762489549)
XLA Ops:
  0.0 41.5 %flow_gradient.1 = f32[4,8,128]{2,1,0:T(8,128)} custom-call(bf16[2,4,128,128]{3,2,1,0:T(8,128)(2,1)} %fwd_in.1, s32[1,16384]{1,0:T(1,128)} %bitcast.1, f32[2,16384]{1,0:T(2,128)} %res.1, s32[4,128,128]{2,1,0:T(8,128)} %labels_in.1, f32[4,128,128]{2,1,0:T(8,128)} %flow_in.1, s32[2]{0:T(128)} %index.1, f32[5]{0:T(128)} %dtab.1, f32[5]{0:T(128)} %atab.1, ...), custom_call_target="tpu_custom_call" | custom-call | tf_op jit(solution)/shard_map/flow_gradient/pallas_call | solution.py:334
  41.5 1.3 %copy.12 = f32[4,8,128]{2,1,0:T(8,128)} copy(f32[4,8,128]{2,1,0:T(8,128)} %flow_gradient.1) | data formatting | bytes 32768

commit v5 on v4

--- a/solution.py
+++ b/solution.py
@@ -17,7 +17,7 @@
 RHO2 = 1.0 / (2.0 * SIGMA - RHO1)
 
 N = 128
-CHUNK = 8192
+CHUNK = 4096
 MESH = pl.DeviceIdType.MESH
 F32 = jnp.float32
 BF16 = jnp.bfloat16
@@ -75,6 +75,9 @@
                 to_down, from_above, send.at[1], receive.at[1],
                 device_id={"depth": down}, device_id_type=MESH),
         )
+        return pair
+
+    def launch(pair):
         pl.when(inside_high)(pair[0].start)
         pl.when(inside_low)(pair[1].start)
         return pair
@@ -134,27 +137,21 @@
             onehot, rt[:, pl.ds(start, CHUNK)], (((1,), (1,)), ((), ())),
             preferred_element_type=F32)
 
-    def run(begin, end, wanted, fresh):
+    def run(wanted, fresh, at, act):
         def step(chunk, carry):
+            pl.when(chunk == at)(act)
             select(chunk, wanted, fresh)
             return carry
-        lax.fori_loop(begin, end, step, 0)
+        lax.fori_loop(0, count // CHUNK, step, 0)
 
     def source(slot, p):
         rows = slice(slot * N, (slot + 1) * N)
         return acc[rows, p * N:(p + 1) * N] + acc[rows, (pairs + p) * N:(pairs + p + 1) * N]
 
-    chunks = count // CHUNK
     ends = (0, planes - 1)
     inner = tuple(range(1, planes - 1))
     below, above = planes, planes + 1
 
-    acc[...] = jnp.zeros_like(acc)
-    run(0, 1, ends, True)
-    pl.semaphore_wait(
-        barrier, groups - 1 + jnp.minimum(z, 1) + jnp.minimum(depths - 1 - z, 1))
-    for copy in loads[:2]:
-        copy.wait()
     half = N // 2
     mine = pl.ds(pl.multiple_of(lax.rem(me, 2) * half, half), half)
     twin = me + 1 - 2 * lax.rem(me, 2)
@@ -164,11 +161,22 @@
     sent_flow = shift(
         flow.at[planes - 1, mine], flow_h.at[0, mine],
         flow.at[0, mine], flow_h.at[1, mine], flow_s, flow_r)
-    run(1, chunks, ends, True)
+
+    def enter():
+        pl.semaphore_wait(
+            barrier, groups - 1 + jnp.minimum(z, 1) + jnp.minimum(depths - 1 - z, 1))
+        for copy in loads[:2]:
+            copy.wait()
+        launch(sent_labels)
+        launch(sent_flow)
+
+    acc[...] = jnp.zeros_like(acc)
+    run(ends, True, 1, enter)
     for slot in range(2):
         for p in range(pairs):
             src[slot, p] = source(slot, p)
-    sent_src = shift(src.at[1], src_h.at[0], src.at[0], src_h.at[1], src_s, src_r)
+    sent_src = launch(shift(
+        src.at[1], src_h.at[0], src.at[0], src_h.at[1], src_s, src_r))
 
     lane = lax.broadcasted_iota(jnp.int32, (N, N), 1)
     row = lax.broadcasted_iota(jnp.int32, (N, N), 0)
@@ -240,9 +248,6 @@
         coefficients(k, diff[k], diff[k - 1], diff[k + 1], labels[k], flow[k])
 
     acc[...] = jnp.zeros_like(acc)
-    run(0, chunks // 2, inner, False)
-    settle_halo(sent_labels)
-    settle_halo(sent_flow)
     relays = [
         pltpu.make_async_remote_copy(
             ref, ref, pass_s.at[slot], pass_r.at[slot],
@@ -258,13 +263,17 @@
                 for copy in pair:
                     act(copy)
 
-    each_relay(lambda copy: copy.start())
-    run(chunks // 2, chunks, inner, False)
+    def hand_over():
+        settle_halo(sent_labels)
+        settle_halo(sent_flow)
+        each_relay(lambda copy: copy.start())
+
+    run(inner, False, 2, hand_over)
     for slot, k in enumerate(inner):
         for p in range(pairs):
             d0[k, p] = source(slot, p) * inv[k, p] * (1.0 / CENTRE)
-    sent_far = shift(
-        d0.at[planes - 2], d0_far.at[0], d0.at[1], d0_far.at[1], far_s, far_r)
+    sent_far = launch(shift(
+        d0.at[planes - 2], d0_far.at[0], d0.at[1], d0_far.at[1], far_s, far_r))
 
     each_relay(lambda copy: copy.wait())
     halo = [[lookup(dtab, lab_h[s, i], dtab.shape[0]) for i in range(2)] for s in range(2)]

time: 43 us -> 36.6 us (0.85)
  Pallas kernels: 41.5 us -> 35 us
    pallas_call x1, Pallas kernels: 41.5 us -> 35 us  [body(): pl.pallas_call(functools.partial(kernel, groups, depths), out_shape=jax.S...]
where the time goes in v5:
time: 36.6 us; the launch traced here: 36.4 us
  Pallas kernels  35 us (96%)
  local copies, waits for them, and re-layouts  1.32 us (4%)
    pallas_call x1, Pallas kernels, body(): pl.pallas_call(functools.partial(kernel, groups, depths), out_shape=jax.S...  35 us
    unnamed x1, local copies, waits for them, and re-layouts  1.32 us

profile of v5, /device:TPU:17, one launch (start us, length us, event | category | flops | bytes accessed | tf_op | source)
XLA Modules:
  0.0 36.4 jit_solution(12657433221345899700)
XLA Ops:
  0.0 35.0 %flow_gradient.1 = f32[4,8,128]{2,1,0:T(8,128)} custom-call(bf16[2,4,128,128]{3,2,1,0:T(8,128)(2,1)} %fwd_in.1, s32[1,16384]{1,0:T(1,128)} %bitcast.1, f32[2,16384]{1,0:T(2,128)} %res.1, s32[4,128,128]{2,1,0:T(8,128)} %labels_in.1, f32[4,128,128]{2,1,0:T(8,128)} %flow_in.1, s32[2]{0:T(128)} %index.1, f32[5]{0:T(128)} %dtab.1, f32[5]{0:T(128)} %atab.1, ...), custom_call_target="tpu_custom_call" | custom-call | tf_op jit(solution)/shard_map/flow_gradient/pallas_call | solution.py:343
  35.0 1.3 %copy.12 = f32[4,8,128]{2,1,0:T(8,128)} copy(f32[4,8,128]{2,1,0:T(8,128)} %flow_gradient.1) | data formatting | bytes 32768

commit v6 on v5

--- a/solution.py
+++ b/solution.py
@@ -308,14 +308,22 @@
     for slot, k in enumerate(inner):
         part[slot] = finish(k)
     sums = scatter(0, 0, len(inner))
+    blank = jnp.zeros((N, N), F32)
+    for p in range(pairs):
+        advance(below, p, gather(d0, below, p, blank, gz[0], blank, d0[0, p]))
+        advance(above, p, gather(d0, above, p, gz[planes], blank, d0[planes - 1, p], blank))
+    sides = ((0, below, gz[planes + 1] * gz[0]), (planes - 1, above, gz[planes + 2] * gz[planes]))
+    for slot, (k, beyond, faces) in enumerate(sides):
+        part[len(inner) + slot] = finish(k)
+        for p in range(pairs):
+            coef = -(wgt[index[p]] * taus[p]) * (4.0 * RHO1 * RHO2 / HALF / HALF)
+            src[slot, p] = coef * fwd[p, k].astype(F32) * faces * (inv[k, p] * inv[beyond, p])
     settle_halo(sent_far)
-    for p in range(pairs):
-        advance(below, p, gather(
-            d0, below, p, gz[planes + 1], gz[0], d0_far[0, p], d0[0, p]))
-        advance(above, p, gather(
-            d0, above, p, gz[planes], gz[planes + 2], d0[planes - 1, p], d0_far[1, p]))
-    for slot, k in enumerate(ends):
-        part[len(inner) + slot] = finish(k)
+    for slot in range(2):
+        total = part[len(inner) + slot]
+        for p in range(pairs):
+            total = total + src[slot, p] * d0_far[slot, p]
+        part[len(inner) + slot] = total
     sums += scatter(1, len(inner), planes)
     for copy in sums:
         copy.wait()

time: 36.6 us -> 35.6 us (0.973)
  Pallas kernels: 35 us -> 34.1 us
    pallas_call x1, Pallas kernels: 35 us -> 34.1 us  [body(): pl.pallas_call(functools.partial(kernel, groups, depths), out_shape=jax.S...]
where the time goes in v6:
time: 35.6 us; the launch traced here: 35.4 us
  Pallas kernels  34.1 us (96%)
  local copies, waits for them, and re-layouts  1.32 us (4%)
    pallas_call x1, Pallas kernels, body(): pl.pallas_call(functools.partial(kernel, groups, depths), out_shape=jax.S...  34.1 us
    unnamed x1, local copies, waits for them, and re-layouts  1.32 us

profile of v6, /device:TPU:17, one launch (start us, length us, event | category | flops | bytes accessed | tf_op | source)
XLA Modules:
  0.0 35.4 jit_solution(3019493349717908574)
XLA Ops:
  0.0 34.1 %flow_gradient.1 = f32[4,8,128]{2,1,0:T(8,128)} custom-call(bf16[2,4,128,128]{3,2,1,0:T(8,128)(2,1)} %fwd_in.1, s32[1,16384]{1,0:T(1,128)} %bitcast.1, f32[2,16384]{1,0:T(2,128)} %res.1, s32[4,128,128]{2,1,0:T(8,128)} %labels_in.1, f32[4,128,128]{2,1,0:T(8,128)} %flow_in.1, s32[2]{0:T(128)} %index.1, f32[5]{0:T(128)} %dtab.1, f32[5]{0:T(128)} %atab.1, ...), custom_call_target="tpu_custom_call" | custom-call | tf_op jit(solution)/shard_map/flow_gradient/pallas_call | solution.py:351
  34.1 1.3 %copy.12 = f32[4,8,128]{2,1,0:T(8,128)} copy(f32[4,8,128]{2,1,0:T(8,128)} %flow_gradient.1) | data formatting | bytes 32768
